TPU v7x, 32 devices: a whole 2x2x4 slice. The times are simulated.
32 devices in a mesh: field: 2 (over core), sx: 4 (over y, x), sy: 4 (over z).
Axes of the slice: x: 2, y: 2, z: 4, core: 2. Of those that a mesh axis runs over, the one named last changes fastest.
Arguments:
- inner_block: bfloat16 [4, 40, 8, 128, 128], P('field', 'sx', 'sy'), may hold values from 0.0004 to 0.03, as said below
- east_block: bfloat16 [4, 40, 8, 128, 128], P('field', 'sx', 'sy'), may hold values from 0.0004 to 0.03, as said below
- north_block: bfloat16 [4, 40, 8, 128, 128], P('field', 'sx', 'sy'), may hold values from 0.0004 to 0.03, as said below
- shift_diag: float32 [4, 40, 8, 128], P('field', 'sx', 'sy'), may hold values from 0.2 to 2
- coupling: float32 [4, 4, 40, 8, 128], P('field', None, 'sx', 'sy'), may hold values from -4 to 4
- coarse_flags: int32 [4, 40, 8, 128], P('field', 'sx', 'sy'), may hold values from 0 to 1, as said below
Outputs:
- coarse_node: bfloat16 [4, 4, 40, 8, 128, 128], P('field', None, 'sx', 'sy')
- coarse_east: bfloat16 [4, 40, 8, 128, 128], P('field', 'sx', 'sy')
- coarse_north: bfloat16 [4, 40, 8, 128, 128], P('field', 'sx', 'sy')
Inputs may be any that keep to these rules, and one draw needn't show every extreme that they name: `coarse_flags`: 1 marks a coarse point of its field; the share of coarse points is drawn for each tile and field. `inner_block`: positive magnitudes. `east_block`: positive magnitudes. `north_block`: positive magnitudes.
All inputs are finite; a program needn't handle non-finite values.
Results may differ from a plain program's by a relative error of at most 0.0046.
Values may be sent and summed in bfloat16 or wider, within the bound.
No kernel may reach another device: no remote copies, remote signals or barrier semaphores. Data moves between devices by JAX's collectives and lax.ppermute only.
A program may use at most 128 MiB of HBM per device.

v0:
```python
import jax
import jax.numpy as jnp
from jax import lax
from jax.sharding import PartitionSpec as P


def from_behind(array, axis, by):
    devices = lax.axis_size(axis)
    pairs = [(i, i + by) for i in range(devices) if 0 <= i + by < devices]
    return lax.ppermute(array, axis, pairs)


def interpolate(matrix, shift, flags):
    tile_nodes = matrix.shape[-1]
    unit = jnp.eye(tile_nodes, dtype=bool)
    offdiag = jnp.where(unit, jnp.zeros((), matrix.dtype), matrix)
    weights = offdiag.astype(jnp.float32)
    coarse = flags.astype(jnp.float32)
    row_total = jnp.sum(weights, axis=-1)
    strong = jnp.sum(weights * coarse[..., None, :], axis=-1)
    diagonal = row_total + shift
    scaling = row_total / jnp.maximum(strong, row_total / 32.0)
    factor = (1.0 - coarse) * scaling / diagonal
    result = (
        coarse[..., :, None] * unit.astype(jnp.float32)
        + factor[..., :, None] * coarse[..., None, :] * weights
    )
    return (result.astype(jnp.bfloat16), offdiag, diagonal)


def neighbour_block(interp, coupling_block, neighbour_interp):
    image = jnp.einsum(
        "fxyik,fxykj->fxyij", coupling_block, neighbour_interp, preferred_element_type=jnp.float32
    ).astype(jnp.bfloat16)
    return (
        -jnp.einsum("fxyia,fxyib->fxyab", interp, image, preferred_element_type=jnp.float32)
    ).astype(jnp.bfloat16)


def body(inner_block, east_block, north_block, shift_diag, coupling, coarse_flags):
    field_count = inner_block.shape[0]
    interp, offdiag, diagonal = interpolate(inner_block, shift_diag, coarse_flags)
    first_field = lax.axis_index("field") * field_count
    row_fields = first_field + jnp.arange(field_count, dtype=jnp.int32)
    own_term = diagonal[..., None] * interp.astype(jnp.float32) - jnp.einsum(
        "fxyik,fxykj->fxyij", offdiag, interp, preferred_element_type=jnp.float32
    )
    column_interp = lax.all_gather(interp, "field", axis=0, tiled=True)
    members = column_interp.shape[0]
    same_field = row_fields[:, None] == jnp.arange(members, dtype=jnp.int32)[None, :]
    weighted = jnp.where(same_field[:, :, None, None, None, None], own_term[:, None], 0.0)
    weighted = (weighted + coupling[..., None] * column_interp[None].astype(jnp.float32)).astype(
        jnp.bfloat16
    )
    coarse_node = jnp.einsum(
        "fxyia,fgxyib->fgxyab", interp, weighted, preferred_element_type=jnp.float32
    ).astype(jnp.bfloat16)
    east_rim = from_behind(interp[:, :1], "sx", -1)
    north_rim = from_behind(interp[:, :, :1], "sy", -1)
    east_interp = jnp.concatenate([interp[:, 1:], east_rim], axis=1)
    north_interp = jnp.concatenate([interp[:, :, 1:], north_rim], axis=2)
    coarse_east = neighbour_block(interp, east_block, east_interp)
    coarse_north = neighbour_block(interp, north_block, north_interp)
    return (coarse_node, coarse_east, coarse_north)


def solution(mesh):
    in_specs = (
        P("field", "sx", "sy", None, None),
        P("field", "sx", "sy", None, None),
        P("field", "sx", "sy", None, None),
        P("field", "sx", "sy", None),
        P("field", None, "sx", "sy", None),
        P("field", "sx", "sy", None),
    )
    out_specs = (
        P("field", None, "sx", "sy", None, None),
        P("field", "sx", "sy", None, None),
        P("field", "sx", "sy", None, None),
    )
    return jax.shard_map(body, mesh=mesh, in_specs=in_specs, out_specs=out_specs, check_vma=False)
```

profile of v0, /device:TPU:28, one launch (start us, length us, event | category | flops | bytes accessed | tf_op | source)
XLA Modules:
  0.0 75.4 jit_solution(13708076331726795222)
XLA Ops:
  7.2 0.0 copy-start
  7.2 0.0 all-gather.2.cloned.1.call-start
  7.2 0.8 %convert_element_type.47 = f32[2,10,2,128]{3,2,1,0:T(2,128)S(1)} convert(s32[2,10,2,128]{3,2,1,0:T(2,128)} %param.11) | non-fusion elementwise | flops 5120 | bytes 40960 | tf_op jit(solution)/shard_map/convert_element_type | solution.py:18
  8.1 2.4 %fusion.6 = (f32[2,10,2,128]{3,2,1,0:T(2,128)S(1)}, f32[2,10,2,128]{3,2,1,0:T(2,128)S(1)}) fusion(f32[2,10,2,128]{3,2,1,0:T(2,128)S(1)} %convert_element_type.47, bf16[2,10,2,128,128]{4,3,2,1,0:T(8,128)(2,1)} %param.6, pred[128,128]{1,0:T(8,128)(4,1)S(1)} %get-tuple-element.15), kind=kLoop, calls=%fused_computation.11 | loop fusion | flops 3266560 | bytes 1388544 | tf_op jit(solution)/shard_map/reduce_sum | solution.py:20
  10.5 0.8 %multiply_divide_fusion = (f32[2,10,2,128]{3,2,1,0:T(2,128)S(1)}, f32[2,10,2,128]{3,2,1,0:T(2,128)S(1)}) fusion(f32[2,10,2,128]{3,2,1,0:T(2,128)S(1)} %get-tuple-element.10, f32[2,10,2,128]{3,2,1,0:T(2,128)S(1)} %get-tuple-element.9, s32[2,10,2,128]{3,2,1,0:T(2,128)} %param.11, f32[2,10,2,128]{3,2,1,0:T(2,128)} %param.9), kind=kLoop, calls=%fused_computation.29 | loop fusion | flops 40960 | bytes 122880 | tf_op jit(solution)/shard_map/div | solution.py:23
  11.3 4.3 %fusion.8 = bf16[2,10,2,128,128]{4,3,2,1,0:T(8,128)(2,1)} fusion(f32[2,10,2,128]{3,2,1,0:T(2,128)S(1)} %get-tuple-element.11, f32[2,10,2,128]{3,2,1,0:T(2,128)S(1)} %convert_element_type.47, f32[128,128]{1,0:T(8,128)S(1)} %get-tuple-element.16, bf16[2,10,2,128,128]{4,3,2,1,0:T(8,128)(2,1)} %param.6, pred[128,128]{1,0:T(8,128)(4,1)S(1)} %get-tuple-element.15), kind=kLoop, calls=%fused_computation.13 | loop fusion | flops 4587520 | bytes 2744320 | tf_op jit(solution)/shard_map/convert_element_type | solution.py:28
  15.6 0.0 copy-start.1
  15.6 0.0 all-gather.2.cloned.1.call-update
  15.7 2.4 %fusion.34 = (bf16[2,10,1,128,128]{4,3,2,1,0:T(8,128)(2,1)S(1)}, bf16[2,10,1,128,128]{4,3,2,1,0:T(8,128)(2,1)}) fusion(bf16[2,10,2,128,128]{4,3,2,1,0:T(8,128)(2,1)} %fusion.8), kind=kLoop, calls=%fused_computation.37 | loop fusion | bytes 2621440 | tf_op jit(solution)/shard_map/slice | solution.py:61
  18.1 3.2 %collective-permute-start.1 = (bf16[2,10,1,128,128]{4,3,2,1,0:T(8,128)(2,1)}, bf16[2,10,1,128,128]{4,3,2,1,0:T(8,128)(2,1)}, u32[]{:S(2)}, u32[]{:S(2)}) collective-permute-start(bf16[2,10,1,128,128]{4,3,2,1,0:T(8,128)(2,1)} %get-tuple-element.14), channel_id=1, source_target_pairs={{1,0},{2,1},{3,2},{5,4},{6,5},{7,6},{9,8},{10,9},{11,10},{13,12},{... | collective-permute-start | bytes 1966088 | tf_op jit(solution)/shard_map/ppermute | solution.py:10
  21.2 0.0 copy-done.1
  21.3 0.7 slice.17
  21.9 3.3 %collective-permute-start = (bf16[2,1,2,128,128]{4,3,2,1,0:T(8,128)(2,1)}, bf16[2,1,2,128,128]{4,3,2,1,0:T(8,128)(2,1)}, u32[]{:S(2)}, u32[]{:S(2)}) collective-permute-start(bf16[2,1,2,128,128]{4,3,2,1,0:T(8,128)(2,1)} %slice.17), channel_id=1, source_target_pairs={{4,0},{8,4},{12,8},{5,1},{9,5},{13,9},{6,2},{10,6},{14,10},{7,3},{... | collective-permute-start | bytes 393224 | tf_op jit(solution)/shard_map/ppermute | solution.py:10
  25.3 7.0 %multiply_subtract_fusion = f32[2,10,2,128,128]{4,3,2,1,0:T(8,128)} fusion(f32[2,10,2,128]{3,2,1,0:T(2,128)S(1)} %get-tuple-element.12, bf16[2,10,2,128,128]{4,3,2,1,0:T(8,128)(2,1)} %param.6, pred[128,128]{1,0:T(8,128)(4,1)S(1)} %get-tuple-element.15, f32[2,10,2,128]{3,2,1,0:T(2,128)S(1)} %convert_element_type.47, ...), kind=kOutput, calls=%fused_computation.16 | convolution fusion | flops 179568640 | bytes 4075520 | tf_op jit(solution)/shard_map/fxyik,fxykj->fxyij/dot_general | solution.py:45
  32.3 1.1 %slice.16 = bf16[2,9,2,128,128]{4,3,2,1,0:T(8,128)(2,1)} slice(bf16[2,10,2,128,128]{4,3,2,1,0:T(8,128)(2,1)S(1)} %copy-done.1), slice={[0:2], [1:10], [0:2], [0:128], [0:128]} | slice | bytes 2359296 | tf_op jit(solution)/shard_map/slice | solution.py:60
  33.3 0.0 copy-start.2
  33.3 3.3 %copy.15 = f32[2,10,2,128,128]{3,4,2,1,0:T(8,128)} copy(f32[2,10,2,128,128]{4,3,2,1,0:T(8,128)} %multiply_subtract_fusion) | data formatting | bytes 5242880 | tf_op jit(solution)/shard_map/sub | solution.py:45
  36.7 0.9 %copy.16 = f32[2,4,10,2,128]{4,1,3,2,0:T(4,128)S(1)} copy(f32[2,4,10,2,128]{4,3,2,1,0:T(2,128)} %param.10) | data formatting | bytes 163840 | tf_op args[4]
  37.6 0.1 iota_compare_fusion.1
  37.6 0.0 collective-permute-done
  37.7 0.0 copy-done
  37.7 0.0 copy-done.2
  37.7 5.3 %negate_convert_fusion.1 = bf16[2,10,2,128,128]{4,3,2,1,0:T(8,128)(2,1)} fusion(bf16[2,10,2,128,128]{4,3,2,1,0:T(8,128)(2,1)S(1)} %copy-done, bf16[2,1,2,128,128]{4,3,2,1,0:T(8,128)(2,1)} %collective-permute-done, bf16[2,9,2,128,128]{4,3,2,1,0:T(8,128)(2,1)} %slice.16, f32[2,10,2,128]{3,2,1,0:T(2,128)S(1)} %get-tuple-element.11, ...), kind=kOutput, calls=%fused_computation.15 | convolution fusion | flops 342753280 | bytes 5365760 | tf_op jit(solution)/shard_map/fxyia,fxyib->fxyab/dot_general | solution.py:36
  42.9 0.0 collective-permute-done.1
  43.0 5.4 %negate_convert_fusion = bf16[2,10,2,128,128]{4,3,2,1,0:T(8,128)(2,1)} fusion(bf16[2,10,2,128,128]{4,3,2,1,0:T(8,128)(2,1)} %param.8, bf16[2,10,1,128,128]{4,3,2,1,0:T(8,128)(2,1)} %collective-permute-done.1, bf16[2,10,1,128,128]{4,3,2,1,0:T(8,128)(2,1)S(1)} %get-tuple-element.13, f32[2,10,2,128]{3,2,1,0:T(2,128)S(1)} %get-tuple-element.11, ...), kind=kOutput, calls=%fused_computation.14 | convolution fusion | flops 342753280 | bytes 5365760 | tf_op jit(solution)/shard_map/fxyia,fxyib->fxyab/dot_general | solution.py:36
  48.4 0.0 all-gather.2.cloned.1.call-done
  48.4 4.9 %copy.17 = f32[4,10,2,128,128]{3,4,0,2,1:T(8,128)} copy(bf16[4,10,2,128,128]{4,3,2,1,0:T(8,128)(2,1)} %all-gather.2.cloned.1.call-done) | data formatting | bytes 7864320 | tf_op jit(solution)/shard_map/convert_element_type | solution.py:52
  53.3 7.3 %convert_bitcast_fusion = bf16[2,4,10,2,128,128]{4,5,1,3,2,0:T(8,128)(2,1)} fusion(f32[4,10,2,128,128]{3,4,0,2,1:T(8,128)} %copy.17, f32[2,4,10,2,128]{4,1,3,2,0:T(4,128)S(1)} %copy.16, f32[2,10,2,128,128]{3,4,2,1,0:T(8,128)} %copy.15, pred[2,4]{1,0:T(4,128)(4,1)S(1)} %iota_compare_fusion.1, f32[2,10,2,128]{3,2,1,0:T(2,128)S(1)} %get-tuple-element.11, ...), kind=kOutput, calls=%fused_computation.2 | convolution fusion | flops 688783360 | bytes 14622728 | tf_op jit(solution)/shard_map/fxyia,fgxyib->fgxyab/dot_general | solution.py:55
  60.6 7.9 %copy.20 = bf16[2,4,10,2,128,128]{5,4,3,2,1,0:T(8,128)(2,1)} copy(bf16[2,4,10,2,128,128]{4,5,1,3,2,0:T(8,128)(2,1)} %convert_bitcast_fusion) | data formatting | bytes 10485760
  (2 shorter events, 0.0 us)
Async XLA Ops:
  7.2 30.5 %copy-start = (bf16[2,10,2,128,128]{4,3,2,1,0:T(8,128)(2,1)S(1)}, bf16[2,10,2,128,128]{4,3,2,1,0:T(8,128)(2,1)}, u32[]{:S(2)}) copy-start(bf16[2,10,2,128,128]{4,3,2,1,0:T(8,128)(2,1)} %param.7) | copy-start | bytes 3932164
  7.2 41.2 %all-gather.2.cloned.1.call-start = ((), (), s32[]{:S(2)}) async-start(), calls=%async_computation | async-start | bytes 3932160 | tf_op jit(solution)/shard_map/all_gather | solution.py:48
  15.6 5.6 %copy-start.1 = (bf16[2,10,2,128,128]{4,3,2,1,0:T(8,128)(2,1)S(1)}, bf16[2,10,2,128,128]{4,3,2,1,0:T(8,128)(2,1)}, u32[]{:S(2)}) copy-start(bf16[2,10,2,128,128]{4,3,2,1,0:T(8,128)(2,1)} %fusion.8) | copy-start | bytes 3932164
  18.1 24.9 %collective-permute-start.1 = (bf16[2,10,1,128,128]{4,3,2,1,0:T(8,128)(2,1)}, bf16[2,10,1,128,128]{4,3,2,1,0:T(8,128)(2,1)}, u32[]{:S(2)}, u32[]{:S(2)}) collective-permute-start(bf16[2,10,1,128,128]{4,3,2,1,0:T(8,128)(2,1)} %get-tuple-element.14), channel_id=1, source_target_pairs={{1,0},{2,1},{3,2},{5,4},{6,5},{7,6},{9,8},{10,9},{11,10},{13,12},{... | collective-permute-start | bytes 1966088 | tf_op jit(solution)/shard_map/ppermute | solution.py:10
  21.9 15.7 %collective-permute-start = (bf16[2,1,2,128,128]{4,3,2,1,0:T(8,128)(2,1)}, bf16[2,1,2,128,128]{4,3,2,1,0:T(8,128)(2,1)}, u32[]{:S(2)}, u32[]{:S(2)}) collective-permute-start(bf16[2,1,2,128,128]{4,3,2,1,0:T(8,128)(2,1)} %slice.17), channel_id=1, source_target_pairs={{4,0},{8,4},{12,8},{5,1},{9,5},{13,9},{6,2},{10,6},{14,10},{7,3},{... | collective-permute-start | bytes 393224 | tf_op jit(solution)/shard_map/ppermute | solution.py:10
  33.3 4.3 %copy-start.2 = (bf16[2,10,2,128,128]{4,3,2,1,0:T(8,128)(2,1)S(1)}, bf16[2,10,2,128,128]{4,3,2,1,0:T(8,128)(2,1)}, u32[]{:S(2)}) copy-start(bf16[2,10,2,128,128]{4,3,2,1,0:T(8,128)(2,1)} %param.6) | copy-start | bytes 3932164
Sparse Core Ops, SparseCore 0:
  15.8 12.5 all-gather.1
where the time goes:
time: 76.1 us; the launch traced here: 75.4 us
  matrix products  25.1 us (33%)
  local copies, waits for them, and re-layouts  21.2 us (28%)
  between operations  14.1 us (19%)
  other arithmetic  8.48 us (11%)
  starting transfers between devices  6.56 us (9%)
    dot_general x2, matrix products, neighbour_block(): jnp.einsum('fxyia,fxyib->fxyab', interp, image, preferred_element_type=jn...  10.7 us
    unnamed x8, local copies, waits for them, and re-layouts  8.83 us
    dot_general x1, matrix products, body(): jnp.einsum('fxyia,fgxyib->fgxyab', interp, weighted, preferred_element_ty...  7.32 us
    dot_general x1, matrix products, body(): jnp.einsum('fxyik,fxykj->fxyij', offdiag, interp, preferred_element_type=...  6.99 us
    ppermute x2, starting transfers between devices, from_behind(): return lax.ppermute(array, axis, pairs)  6.52 us
    convert_element_type x1, local copies, waits for them, and re-layouts, body(): column_interp[None].astype(jnp.float32)  4.89 us
    convert_element_type x1, other arithmetic, interpolate(): return (result.astype(jnp.bfloat16), offdiag, diagonal)  4.34 us
    sub x1, local copies, waits for them, and re-layouts, body(): diagonal[..., None] * interp.astype(jnp.float32)  3.31 us
  transfers between devices with their start and end apart: 3, of which 0 were waited for; matrix products, arithmetic and copies ran while one was open for 35% of the time, Pallas kernels for 0%

commit v1 on v0

v1 whole, which is shorter than its diff:
```python
import jax
import jax.numpy as jnp
from jax import lax
from jax.experimental import pallas as pl
from jax.experimental.pallas import tpu as pltpu
from jax.sharding import PartitionSpec as P

BF = jnp.bfloat16
F32 = jnp.float32
ANY = pl.BlockSpec(memory_space=pl.ANY)


def nn(left, right):
    return lax.dot_general(left, right, (((1,), (0,)), ((), ())), preferred_element_type=F32)


def nt(left, right):
    return lax.dot_general(left, right, (((1,), (1,)), ((), ())), preferred_element_type=F32)


def iota(shape, dim):
    return lax.broadcasted_iota(jnp.int32, shape, dim)


def round_up(value, step):
    return -(-value // step) * step


def one_hot(key_row, rows):
    m = key_row.shape[-1]
    hit = iota((rows, m), 0).astype(F32) == jnp.broadcast_to(key_row, (rows, m))
    return jnp.where(hit, 1.0, 0.0).astype(BF)


def interp_kernel(y_lo, y_hi, pack, shape, *refs):
    nf, nx, ny, m = shape
    tiles = [(f, x, y) for x in range(nx) for f in range(nf) for y in range(y_lo, y_hi)]
    count = len(tiles)
    half = m // 2
    if pack:
        w_hbm, s_hbm, c_hbm, p_hbm, a_hbm, z_hbm = refs[:6]
        wv, sv, cv, pv, av, fscr, cscr, insem, outsem, zv, kscr = refs[6:]
    else:
        w_hbm, s_hbm, c_hbm, _, p_hbm, a_hbm = refs[:6]
        wv, sv, cv, pv, av, fscr, cscr, insem, outsem = refs[6:]
    c_copy = pltpu.make_async_copy(c_hbm, cv, insem.at[nx])
    s_copy = pltpu.make_async_copy(s_hbm, sv, insem.at[nx + 1])
    c_copy.start()
    s_copy.start()
    w_copies = []
    for x in range(nx):
        copy = pltpu.make_async_copy(w_hbm.at[:, x, pl.ds(y_lo, y_hi - y_lo)], wv.at[x], insem.at[x])
        copy.start()
        w_copies.append(copy)
    rows = cscr.shape[0]
    cscr[...] = jnp.zeros((rows, m), F32)
    fscr[...] = jnp.zeros(fscr.shape, F32)
    eye = iota((m, m), 0) == iota((m, m), 1)
    off = jnp.where(eye, 0.0, 1.0).astype(BF)
    c_copy.wait()
    for t, (f, x, y) in enumerate(tiles):
        cscr[pl.ds(t, 1), :] = cv[f, x, pl.ds(y, 1), :].astype(F32)
    if pack:
        cs = cscr[...]
        ones = jnp.ones((m, m), BF)
        few = nn(cs.astype(BF), ones) <= half
        sel = jnp.where(few, cs, 1.0 - cs)
        before = jnp.where(iota((m, m), 0) < iota((m, m), 1), 1.0, 0.0).astype(BF)
        rank = nn(sel.astype(BF), before)
        kscr[0] = jnp.where(sel > 0.0, rank, -1.0)
        kscr[1] = jnp.where(few, 1.0, 0.0)
        z_rows = count * half
        zv[pl.ds(z_rows, rows), :] = kscr[0].astype(BF)
        zv[pl.ds(z_rows + rows, rows), :] = kscr[1].astype(BF)
        zv[pl.ds(z_rows + 2 * rows, rows), :] = cs.astype(BF)
    s_copy.wait()
    lhs_top = iota((16, m), 0) < 8
    for t, (f, x, y) in enumerate(tiles):
        if f == 0 and y == y_lo:
            w_copies[x].wait()
        c_row = cscr[pl.ds(t, 1), :]
        lhs = jnp.where(lhs_top, 1.0, jnp.broadcast_to(c_row, (16, m))).astype(BF)
        sums = nt(lhs, wv[x, f, y - y_lo] * off)
        total = sums[0:1, :]
        strong = sums[8:9, :]
        diagonal = total + sv[f, x, pl.ds(y, 1), :]
        scaling = total / jnp.maximum(strong, total / 32.0)
        fscr[pl.ds(t, 1), :] = (1.0 - c_row) * scaling / diagonal
        av[pl.ds(t, 1), :] = diagonal
    columns = jnp.transpose(fscr[...])
    copies = []
    for t, (f, x, y) in enumerate(tiles):
        c_row = cscr[pl.ds(t, 1), :]
        scaled = (wv[x, f, y - y_lo].astype(F32) * c_row) * columns[:, t : t + 1]
        value = jnp.where(eye, jnp.broadcast_to(c_row, (m, m)), scaled)
        pv[x, f, y - y_lo] = value.astype(BF)
        if pack:
            picked = jnp.where(
                jnp.broadcast_to(kscr[1, pl.ds(t, 1), :], (m, m)) > 0.5, jnp.transpose(value), value
            ).astype(BF)
            zv[pl.ds(t * half, half), :] = nn(one_hot(kscr[0, pl.ds(t, 1), :], half), picked).astype(BF)
        if f == nf - 1 and y == y_hi - 1:
            copy = pltpu.make_async_copy(
                pv.at[x], p_hbm.at[:, x, pl.ds(y_lo, y_hi - y_lo)], outsem.at[x]
            )
            copy.start()
            copies.append(copy)
    copy = pltpu.make_async_copy(av, a_hbm, outsem.at[nx])
    copy.start()
    copies.append(copy)
    if pack:
        copy = pltpu.make_async_copy(zv, z_hbm, outsem.at[nx + 1])
        copy.start()
        copies.append(copy)
    for copy in copies:
        copy.wait()


def interp_call(inner, shift, flags, partial, y_lo, y_hi):
    nf, nx, ny, m, _ = inner.shape
    pack = partial is None
    span = y_hi - y_lo
    count = nf * nx * span
    rows = round_up(count, 16)
    p_shape = jax.ShapeDtypeStruct(inner.shape, BF)
    a_shape = jax.ShapeDtypeStruct((rows, m), F32)
    out_shape = [p_shape, a_shape]
    scratch = [
        pltpu.VMEM((nx, nf, span, m, m), BF),
        pltpu.VMEM(shift.shape, F32),
        pltpu.VMEM(flags.shape, jnp.int32),
        pltpu.VMEM((nx, nf, span, m, m), BF),
        pltpu.VMEM((rows, m), F32),
        pltpu.VMEM((round_up(rows, m), m), F32),
        pltpu.VMEM((rows, m), F32),
        pltpu.SemaphoreType.DMA((nx + 2,)),
        pltpu.SemaphoreType.DMA((nx + 2,)),
    ]
    operands = [inner, shift, flags]
    aliases = {}
    if pack:
        z_rows = count * (m // 2) + 3 * rows
        out_shape.append(jax.ShapeDtypeStruct((z_rows, m), BF))
        scratch += [pltpu.VMEM((z_rows, m), BF), pltpu.VMEM((2, rows, m), F32)]
    else:
        operands.append(partial)
        aliases = {3: 0}

    def kernel(*refs):
        interp_kernel(y_lo, y_hi, pack, (nf, nx, ny, m), *refs)

    return pl.pallas_call(
        kernel,
        out_shape=out_shape,
        in_specs=[ANY] * len(operands),
        out_specs=[ANY] * len(out_shape),
        scratch_shapes=scratch,
        input_output_aliases=aliases,
        name="interp_pack" if pack else "interp_rest",
    )(*operands)


def main_kernel(shape, groups, *refs):
    nf, nx, ny, m = shape
    w_hbm, e_hbm, n_hbm, p_hbm, d_hbm, a0_hbm, a1_hbm = refs[:7]
    q_hbm = refs[7 : 6 + groups]
    refs = refs[6 + groups :]
    node_hbm, east_hbm, north_hbm, ge_hbm, gn_hbm = refs[:5]
    wv, ev, nv, pv, qv, dv, a0v, a1v, ov, eov, nov, gev, gnv, insem, smallsem, osem, rsem = refs[5:]
    me = lax.axis_index("field")
    small = [
        pltpu.make_async_copy(d_hbm, dv, smallsem.at[0]),
        pltpu.make_async_copy(a0_hbm, a0v, smallsem.at[1]),
        pltpu.make_async_copy(a1_hbm, a1v, smallsem.at[2]),
    ]
    for copy in small:
        copy.start()

    def inputs(x):
        pairs = [(p_hbm, pv), (w_hbm, wv), (e_hbm, ev), (n_hbm, nv)]
        copies = [
            pltpu.make_async_copy(src.at[:, x], dst.at[x], insem.at[i, x]) for i, (src, dst) in enumerate(pairs)
        ]
        for k in range(groups - 1):
            copies.append(pltpu.make_async_copy(q_hbm[k].at[:, x], qv.at[k, x], insem.at[4 + k, x]))
        return copies

    def outputs(x):
        copies = []
        for f in range(nf):
            for k in range(groups):
                g = lax.rem(me + k, groups) * nf
                copies.append(
                    pltpu.make_async_copy(
                        ov.at[x, f, k], node_hbm.at[f, pl.ds(g, nf), x], osem.at[f * groups + k, x]
                    )
                )
        if x < nx - 1:
            copies.append(pltpu.make_async_copy(eov.at[x], east_hbm.at[:, x], osem.at[nf * groups, x]))
        copies.append(
            pltpu.make_async_copy(
                nov.at[x], north_hbm.at[:, x, pl.ds(0, ny - 1)], osem.at[nf * groups + 1, x]
            )
        )
        return copies

    for x in range(nx):
        for copy in inputs(x):
            copy.start()
    for copy in small:
        copy.wait()
    off = jnp.where(iota((m, m), 0) == iota((m, m), 1), 0.0, 1.0).astype(BF)
    for copy in inputs(0):
        copy.wait()
    for x in range(nx):
        if x + 1 < nx:
            for copy in inputs(x + 1):
                copy.wait()
        for f in range(nf):
            for y in range(ny):
                a_row = a0v if y == 0 else a1v
                t = x * nf + f if y == 0 else (x * nf + f) * (ny - 1) + y - 1
                pt = jnp.transpose(pv[x, f, y])
                minus = -pt
                both = nn(minus, jnp.concatenate([wv[x, f, y] * off, ev[x, f, y]], axis=1))
                gn = nn(minus, nv[x, f, y]).astype(BF)
                ge = both[:, m:].astype(BF)
                if x + 1 < nx:
                    eov[x, f, y] = nn(ge, pv[x + 1, f, y]).astype(BF)
                else:
                    gev[f, y] = ge
                if y + 1 < ny:
                    nov[x, f, y] = nn(gn, pv[x, f, y + 1]).astype(BF)
                else:
                    gnv[x, f] = gn
                pt32 = pt.astype(F32)
                for k in range(groups):
                    g = lax.rem(me + k, groups) * nf
                    for j in range(nf):
                        row = dv[f, g + j, x, pl.ds(y, 1), :]
                        if k == 0 and j == f:
                            row = row + a_row[pl.ds(t, 1), :]
                            left = (pt32 * row + both[:, :m]).astype(BF)
                        else:
                            left = (pt32 * row).astype(BF)
                        right = pv[x, j, y] if k == 0 else qv[k - 1, x, j, y]
                        ov[x, f, k, j, y] = nn(left, right).astype(BF)
        for copy in outputs(x):
            copy.start()
    rims = [
        pltpu.make_async_copy(gev, ge_hbm, rsem.at[0]),
        pltpu.make_async_copy(gnv, gn_hbm, rsem.at[1]),
    ]
    for copy in rims:
        copy.start()
    for x in range(nx):
        for copy in outputs(x):
            copy.wait()
    for copy in rims:
        copy.wait()


def main_call(inner, east, north, interp, others, coupling, a0, a1):
    nf, nx, ny, m, _ = inner.shape
    groups = len(others) + 1
    tile = (m, m)
    out_shape = [
        jax.ShapeDtypeStruct((nf, groups * nf, nx, ny, m, m), BF),
        jax.ShapeDtypeStruct(inner.shape, BF),
        jax.ShapeDtypeStruct(inner.shape, BF),
        jax.ShapeDtypeStruct((nf, ny, m, m), BF),
        jax.ShapeDtypeStruct((nx, nf, m, m), BF),
    ]
    scratch = [pltpu.VMEM((nx, nf, ny) + tile, BF) for _ in range(4)] + [
        pltpu.VMEM((groups - 1, nx, nf, ny) + tile, BF),
        pltpu.VMEM(coupling.shape, F32),
        pltpu.VMEM(a0.shape, F32),
        pltpu.VMEM(a1.shape, F32),
        pltpu.VMEM((nx, nf, groups, nf, ny) + tile, BF),
        pltpu.VMEM((nx, nf, ny) + tile, BF),
        pltpu.VMEM((nx, nf, ny - 1) + tile, BF),
        pltpu.VMEM((nf, ny) + tile, BF),
        pltpu.VMEM((nx, nf) + tile, BF),
        pltpu.SemaphoreType.DMA((3 + groups, nx)),
        pltpu.SemaphoreType.DMA((3,)),
        pltpu.SemaphoreType.DMA((nf * groups + 2, nx)),
        pltpu.SemaphoreType.DMA((2,)),
    ]
    operands = [inner, east, north, interp, coupling, a0, a1] + list(others)

    def kernel(*refs):
        main_kernel((nf, nx, ny, m), groups, *refs)

    return pl.pallas_call(
        kernel,
        out_shape=out_shape,
        in_specs=[ANY] * len(operands),
        out_specs=[ANY] * len(out_shape),
        scratch_shapes=scratch,
        name="blocks",
    )(*operands)


def rim_kernel(shape, *refs):
    nf, nx, ny, m = shape
    half = m // 2
    east_hbm, north_hbm = refs[6:8]
    ge_hbm, gn_hbm, pe_hbm, z_hbm = refs[:4]
    gev, gnv, pev, zv, eov, nov, insem, osem = refs[8:]
    count = nf * nx
    rows = (z_hbm.shape[0] - count * half) // 3
    loads = [
        pltpu.make_async_copy(ge_hbm, gev, insem.at[0]),
        pltpu.make_async_copy(gn_hbm, gnv, insem.at[1]),
        pltpu.make_async_copy(pe_hbm, pev, insem.at[2]),
        pltpu.make_async_copy(z_hbm, zv, insem.at[3]),
    ]
    for copy in loads:
        copy.start()
    for copy in loads:
        copy.wait()
    stores = []
    for f in range(nf):
        for y in range(ny):
            eov[f, y] = nn(gev[f, y], pev[f, 0, y]).astype(BF)
    stores.append(pltpu.make_async_copy(eov, east_hbm.at[:, nx - 1], osem.at[nx]))
    stores[-1].start()
    base = count * half
    keys = zv[pl.ds(base, rows), :].astype(F32)
    cases = zv[pl.ds(base + rows, rows), :].astype(F32)
    flags = zv[pl.ds(base + 2 * rows, rows), :].astype(F32)
    for x in range(nx):
        for f in range(nf):
            t = x * nf + f
            few = cases[t : t + 1, :]
            few_half = jnp.broadcast_to(few, (half, m)).astype(BF)
            packed = zv[pl.ds(t * half, half), :]
            hot = one_hot(keys[t : t + 1, :], half)
            few_not = (1.0 - few_half.astype(F32)).astype(BF)
            first = packed * few_half + hot * few_not
            second = hot * few_half + packed * few_not
            g = gnv[x, f]
            mid = nt(g, first).astype(BF)
            rest = jnp.broadcast_to(flags[t : t + 1, :] * (1.0 - few), (m, m))
            nov[x, f] = (nn(mid, second) + g.astype(F32) * rest).astype(BF)
        stores.append(pltpu.make_async_copy(nov.at[x], north_hbm.at[:, x, ny - 1], osem.at[x]))
        stores[-1].start()
    for copy in stores:
        copy.wait()


def rim_call(ge, gn, pe, packed, east, north):
    nf, nx, ny, m, _ = east.shape
    operands = [ge, gn, pe, packed, east, north]
    tile = (m, m)
    scratch = [
        pltpu.VMEM(ge.shape, BF),
        pltpu.VMEM(gn.shape, BF),
        pltpu.VMEM(pe.shape, BF),
        pltpu.VMEM(packed.shape, BF),
        pltpu.VMEM((nf, ny) + tile, BF),
        pltpu.VMEM((nx, nf) + tile, BF),
        pltpu.SemaphoreType.DMA((4,)),
        pltpu.SemaphoreType.DMA((nx + 1,)),
    ]

    def kernel(*refs):
        rim_kernel((nf, nx, ny, m), *refs)

    return pl.pallas_call(
        kernel,
        out_shape=[jax.ShapeDtypeStruct(east.shape, BF), jax.ShapeDtypeStruct(north.shape, BF)],
        in_specs=[ANY] * len(operands),
        out_specs=[ANY] * 2,
        scratch_shapes=scratch,
        input_output_aliases={4: 0, 5: 1},
        name="rims",
    )(*operands)


def from_next(array, axis):
    devices = lax.axis_size(axis)
    return lax.ppermute(array, axis, [(i, i - 1) for i in range(1, devices)])


def body(inner_block, east_block, north_block, shift_diag, coupling, coarse_flags):
    ny = inner_block.shape[2]
    partial, a0, packed = interp_call(inner_block, shift_diag, coarse_flags, None, 0, 1)
    north_packed = from_next(packed, "sy")
    interp, a1 = interp_call(inner_block, shift_diag, coarse_flags, partial, 1, ny)
    groups = lax.axis_size("field")
    others = [
        lax.ppermute(interp, "field", [((i + k) % groups, i) for i in range(groups)]) for k in range(1, groups)
    ]
    east_interp = from_next(interp[:, :1], "sx")
    coarse_node, coarse_east, coarse_north, ge, gn = main_call(
        inner_block, east_block, north_block, interp, others, coupling, a0, a1
    )
    coarse_east, coarse_north = rim_call(ge, gn, east_interp, north_packed, coarse_east, coarse_north)
    return (coarse_node, coarse_east, coarse_north)


def solution(mesh):
    in_specs = (
        P("field", "sx", "sy", None, None),
        P("field", "sx", "sy", None, None),
        P("field", "sx", "sy", None, None),
        P("field", "sx", "sy", None),
        P("field", None, "sx", "sy", None),
        P("field", "sx", "sy", None),
    )
    out_specs = (
        P("field", None, "sx", "sy", None, None),
        P("field", "sx", "sy", None, None),
        P("field", "sx", "sy", None, None),
    )
    return jax.shard_map(body, mesh=mesh, in_specs=in_specs, out_specs=out_specs, check_vma=False)
```

time: 76.1 us -> 35.2 us (0.46)
  Pallas kernels: 0 us -> 25.5 us
  matrix products: 25.1 us -> 0 us
  local copies, waits for them, and re-layouts: 21.2 us -> 2.77 us
  between operations: 14.1 us -> 0.74 us
  other arithmetic: 8.48 us -> 0 us
  starting transfers between devices: 6.56 us -> 5.79 us
    pallas_call x0 -> x4, Pallas kernels: none -> 25.5 us  [the longest x1 14 us: main_call(): pl.pallas_call(kernel, out_shape=out_shape, in_specs=[ANY] * len(operands...]
    dot_general x4 -> x0, matrix products: 25.1 us -> none  [the longest x2 10.7 us: neighbour_block(): jnp.einsum('fxyia,fxyib->fxyab', interp, image, preferred_element_type=jn...]
    unnamed x8, local copies, waits for them, and re-layouts: 8.83 us -> 1.85 us
    convert_element_type x2 -> x0, other arithmetic: 5.17 us -> none  [the longest x1 4.34 us: interpolate(): return (result.astype(jnp.bfloat16), offdiag, diagonal)]
    convert_element_type x1 -> x0, local copies, waits for them, and re-layouts: 4.89 us -> none  [body(): column_interp[None].astype(jnp.float32)]
    sub x1 -> x0, local copies, waits for them, and re-layouts: 3.31 us -> none  [body(): diagonal[..., None] * interp.astype(jnp.float32)]
    slice x3 -> x1, local copies, waits for them, and re-layouts: 4.14 us -> 0.92 us  [body(): east_interp = from_next(interp[:, :1], 'sx')]
    reduce_sum x1 -> x0, other arithmetic: 2.43 us -> none  [interpolate(): strong = jnp.sum(weights * coarse[..., None, :], axis=-1)]
  transfers between devices with their start and end apart: 3 -> 3, of which waited for: 0 -> 0; matrix products, arithmetic and copies ran while one was open for 35% -> 3% of each run, Pallas kernels for 0% -> 40%
where the time goes in v1:
time: 35.2 us; the launch traced here: 34.8 us
  Pallas kernels  25.5 us (72%)
  starting transfers between devices  5.79 us (16%)
  local copies, waits for them, and re-layouts  2.77 us (8%)
  between operations  0.74 us (2%)
    pallas_call x1, Pallas kernels, main_call(): pl.pallas_call(kernel, out_shape=out_shape, in_specs=[ANY] * len(operands...  14 us
    pallas_call x2, Pallas kernels, interp_call(): pl.pallas_call(kernel, out_shape=out_shape, in_specs=[ANY] * len(operands...  8.87 us
    ppermute x2, starting transfers between devices, from_next(): return lax.ppermute(array, axis, [(i, i - 1) for i in range(1, devices)])  5.72 us
    pallas_call x1, Pallas kernels, rim_call(): pl.pallas_call(kernel, out_shape=[jax.ShapeDtypeStruct(east.shape, BF), j...  2.68 us
    unnamed x8, local copies, waits for them, and re-layouts  1.85 us
    slice x1, local copies, waits for them, and re-layouts, body(): east_interp = from_next(interp[:, :1], 'sx')  0.92 us
  transfers between devices with their start and end apart: 3, of which 0 were waited for; matrix products, arithmetic and copies ran while one was open for 3% of the time, Pallas kernels for 40%

profile of v1, /device:TPU:28, one launch (start us, length us, event | category | flops | bytes accessed | tf_op | source)
XLA Modules:
  0.0 34.8 jit_solution(17331990058361935215)
XLA Ops:
  0.6 4.7 %interp_pack.1 = (bf16[2,10,2,128,128]{4,3,2,1,0:T(8,128)(2,1)}, f32[32,128]{1,0:T(8,128)}, bf16[1376,128]{1,0:T(8,128)(2,1)}) custom-call(bf16[2,10,2,128,128]{4,3,2,1,0:T(8,128)(2,1)} %refs_0_.5, f32[2,10,2,128]{3,2,1,0:T(2,128)} %refs_1_.4, s32[2,10,2,128]{3,2,1,0:T(2,128)} %refs_2_.4), custom_call_target="tpu_custom_call" | custom-call | tf_op jit(solution)/shard_map/interp_pack/pallas_call | solution.py:152
  5.4 0.0 copy-start.3
  5.4 4.1 %interp_rest.1 = (bf16[2,10,2,128,128]{4,3,2,1,0:T(8,128)(2,1)}, f32[32,128]{1,0:T(8,128)}) custom-call(bf16[2,10,2,128,128]{4,3,2,1,0:T(8,128)(2,1)} %refs_0_.5, f32[2,10,2,128]{3,2,1,0:T(2,128)} %refs_1_.4, s32[2,10,2,128]{3,2,1,0:T(2,128)} %refs_2_.4, bf16[2,10,2,128,128]{4,3,2,1,0:T(8,128)(2,1)} %get-tuple-element.15.refs_3_), custom_call_target="tpu_custom_call", output_to_operand_aliasing={{0}: (3, {})} | custom-call | tf_op jit(solution)/shard_map/interp_rest/pallas_call | solution.py:152
  9.5 0.1 collective-permute-start
  9.6 0.0 copy-done.3
  9.6 2.4 %collective-permute-start.2 = (bf16[1376,128]{1,0:T(8,128)(2,1)S(1)}, bf16[1376,128]{1,0:T(8,128)(2,1)S(1)}, u32[]{:S(2)}, u32[]{:S(2)}) collective-permute-start(bf16[1376,128]{1,0:T(8,128)(2,1)S(1)} %copy-done.3), channel_id=1, source_target_pairs={{1,0},{2,1},{3,2},{5,4},{6,5},{7,6},{9,8},{10,9},{11,10},{13,12},{... | collective-permute-start | bytes 1056776 | tf_op jit(solution)/shard_map/ppermute | solution.py:383
  12.0 0.9 %slice.3 = bf16[2,1,2,128,128]{4,3,2,1,0:T(8,128)(2,1)S(1)} slice(bf16[2,10,2,128,128]{4,3,2,1,0:T(8,128)(2,1)} %get-tuple-element.16.refs_3_), slice={[0:2], [0:1], [0:2], [0:128], [0:128]} | slice | bytes 262144 | tf_op jit(solution)/shard_map/slice | solution.py:395
  12.9 3.3 %collective-permute-start.1 = (bf16[2,1,2,128,128]{4,3,2,1,0:T(8,128)(2,1)S(1)}, bf16[2,1,2,128,128]{4,3,2,1,0:T(8,128)(2,1)S(1)}, u32[]{:S(2)}, u32[]{:S(2)}) collective-permute-start(bf16[2,1,2,128,128]{4,3,2,1,0:T(8,128)(2,1)S(1)} %slice.3), channel_id=1, source_target_pairs={{4,0},{8,4},{12,8},{5,1},{9,5},{13,9},{6,2},{10,6},{14,10},{7,3},{... | collective-permute-start | bytes 393224 | tf_op jit(solution)/shard_map/ppermute | solution.py:383
  16.3 0.0 collective-permute-done.refs_7_
  16.3 0.0 copy-start
  16.3 1.1 %copy-done = bf16[2,10,2,128,128]{4,3,2,1,0:T(8,128)(2,1)} copy-done((bf16[2,10,2,128,128]{4,3,2,1,0:T(8,128)(2,1)}, bf16[2,10,2,128,128]{4,3,2,1,0:T(8,128)(2,1)S(1)}, u32[]{:S(2)}) %copy-start) | copy-done | bytes 1310744
  17.4 14.0 %blocks.1 = (bf16[2,4,10,2,128,128]{5,4,3,2,1,0:T(8,128)(2,1)}, bf16[2,10,2,128,128]{4,3,2,1,0:T(8,128)(2,1)}, bf16[2,10,2,128,128]{4,3,2,1,0:T(8,128)(2,1)}, bf...) custom-call(bf16[2,10,2,128,128]{4,3,2,1,0:T(8,128)(2,1)} %refs_0_.5, bf16[2,10,2,128,128]{4,3,2,1,0:T(8,128)(2,1)} %refs_1_.5, ...), custom_call_target="tpu_custom_call" | custom-call | tf_op jit(solution)/shard_map/blocks/pallas_call | solution.py:294
  31.4 0.0 collective-permute-done.1.refs_2_
  31.4 0.0 copy-start.2
  31.4 0.0 collective-permute-done.2.refs_3_
  31.4 0.0 copy-start.1
  31.4 0.6 %copy-done.2 = bf16[2,1,2,128,128]{4,3,2,1,0:T(8,128)(2,1)} copy-done((bf16[2,1,2,128,128]{4,3,2,1,0:T(8,128)(2,1)}, bf16[2,1,2,128,128]{4,3,2,1,0:T(8,128)(2,1)S(1)}, u32[]{:S(2)}) %copy-start.2) | copy-done | bytes 131096
  32.0 0.1 copy-done.1
  32.1 2.7 %rims.1 = (bf16[2,10,2,128,128]{4,3,2,1,0:T(8,128)(2,1)}, bf16[2,10,2,128,128]{4,3,2,1,0:T(8,128)(2,1)}) custom-call(bf16[2,2,128,128]{3,2,1,0:T(8,128)(2,1)} %get-tuple-element.20.refs_0_, bf16[10,2,128,128]{3,2,1,0:T(8,128)(2,1)} %get-tuple-element.21.refs_1_, ...), custom_call_target="tpu_custom_call", output_to_operand_aliasing={{0}: (4, {}), {1}: (5, {})} | custom-call | tf_op jit(solution)/shard_map/rims/pallas_call | solution.py:370
Async XLA Ops:
  5.4 4.2 %copy-start.3 = (bf16[1376,128]{1,0:T(8,128)(2,1)S(1)}, bf16[1376,128]{1,0:T(8,128)(2,1)}, u32[]{:S(2)}) copy-start(bf16[1376,128]{1,0:T(8,128)(2,1)} %get-tuple-element.22) | copy-start | bytes 1056772
  9.5 6.7 %collective-permute-start = (bf16[2,10,2,128,128]{4,3,2,1,0:T(8,128)(2,1)}, bf16[2,10,2,128,128]{4,3,2,1,0:T(8,128)(2,1)S(1)}, u32[]{:S(2)}, u32[]{:S(2)}) collective-permute-start(bf16[2,10,2,128,128]{4,3,2,1,0:T(8,128)(2,1)} %get-tuple-element.16.refs_3_), channel_id=1, source_target_pairs={{16,0},{0,16},{17,1},{1,17},{18,2},{2,18},{19,3},{3,19},{20,4},{4,... | collective-permute-start | bytes 3932168 | tf_op jit(solution)/shard_map/ppermute | solution.py:393
  9.6 21.8 %collective-permute-start.2 = (bf16[1376,128]{1,0:T(8,128)(2,1)S(1)}, bf16[1376,128]{1,0:T(8,128)(2,1)S(1)}, u32[]{:S(2)}, u32[]{:S(2)}) collective-permute-start(bf16[1376,128]{1,0:T(8,128)(2,1)S(1)} %copy-done.3), channel_id=1, source_target_pairs={{1,0},{2,1},{3,2},{5,4},{6,5},{7,6},{9,8},{10,9},{11,10},{13,12},{... | collective-permute-start | bytes 1056776 | tf_op jit(solution)/shard_map/ppermute | solution.py:383
  12.9 18.4 %collective-permute-start.1 = (bf16[2,1,2,128,128]{4,3,2,1,0:T(8,128)(2,1)S(1)}, bf16[2,1,2,128,128]{4,3,2,1,0:T(8,128)(2,1)S(1)}, u32[]{:S(2)}, u32[]{:S(2)}) collective-permute-start(bf16[2,1,2,128,128]{4,3,2,1,0:T(8,128)(2,1)S(1)} %slice.3), channel_id=1, source_target_pairs={{4,0},{8,4},{12,8},{5,1},{9,5},{13,9},{6,2},{10,6},{14,10},{7,3},{... | collective-permute-start | bytes 393224 | tf_op jit(solution)/shard_map/ppermute | solution.py:383
  16.3 1.1 %copy-start = (bf16[2,10,2,128,128]{4,3,2,1,0:T(8,128)(2,1)}, bf16[2,10,2,128,128]{4,3,2,1,0:T(8,128)(2,1)S(1)}, u32[]{:S(2)}) copy-start(bf16[2,10,2,128,128]{4,3,2,1,0:T(8,128)(2,1)S(1)} %collective-permute-done.refs_7_) | copy-start | bytes 3932164
  31.4 0.7 %copy-start.2 = (bf16[2,1,2,128,128]{4,3,2,1,0:T(8,128)(2,1)}, bf16[2,1,2,128,128]{4,3,2,1,0:T(8,128)(2,1)S(1)}, u32[]{:S(2)}) copy-start(bf16[2,1,2,128,128]{4,3,2,1,0:T(8,128)(2,1)S(1)} %collective-permute-done.1.refs_2_) | copy-start | bytes 393220
  31.4 0.8 %copy-start.1 = (bf16[1376,128]{1,0:T(8,128)(2,1)}, bf16[1376,128]{1,0:T(8,128)(2,1)S(1)}, u32[]{:S(2)}) copy-start(bf16[1376,128]{1,0:T(8,128)(2,1)S(1)} %collective-permute-done.2.refs_3_) | copy-start | bytes 1056772
